TPU v7x, 32 devices: a whole 2x2x4 slice. The times are simulated.
32 devices in a mesh: req: 4 (over z), head: 2 (over core), exp: 4 (over y, x).
Axes of the slice: x: 2, y: 2, z: 4, core: 2. Of those that a mesh axis runs over, the one named last changes fastest.
Arguments:
- queries: bfloat16 [16, 64, 32, 128], P('req', 'exp', 'head'), may hold values from -8 to 8
- new_keys: bfloat16 [16, 64, 4, 128], P('req', 'exp', 'head'), may hold values from -8 to 8
- new_values: bfloat16 [16, 64, 4, 128], P('req', 'exp', 'head'), may hold values from -6 to 6
- key_cache: bfloat16 [16, 24576, 4, 128], P('req', 'exp', 'head'), may hold values from -6 to 6
- value_cache: bfloat16 [16, 24576, 4, 128], P('req', 'exp', 'head'), may hold values from -6 to 6
- lengths: int32 [16], P('req'), may hold values from 1 to 24576, 131072 in all
- residual: bfloat16 [1024, 2048], P(('req', 'exp')), may hold values from -24 to 24
- out_weight: bfloat16 [4096, 2048], P('head', 'exp'), may hold values from -1.796875 to 1.796875
- norm_gain: float32 [2048], replicated, may hold values from 0.1 to 1.9
- route_ids: int32 [1024, 8], P(('req', 'exp')), may hold values from 0 to 15, all different within a row; in each aligned block of 64 rows (0 to 63, 64 to 127, ...) at most 64 rows name the same one
- route_weights: float32 [1024, 8], P(('req', 'exp')), may hold values from 0.05 to 0.3
- expert_in: bfloat16 [16, 2048, 2, 768], P(('req', 'exp'), None, None, 'head'), may hold values from -0.125 to 0.125
- expert_out: bfloat16 [16, 768, 2048], P(('req', 'exp'), 'head'), may hold values from -0.21875 to 0.21875
Outputs:
- output: bfloat16 [1024, 2048], P(('req', 'exp'), 'head')
Inputs may be any that keep to these rules, and one draw needn't show every extreme that they name: `route_ids`: each row names 8 different experts. Among the 64 rows of one device (aligned blocks of rows 0 to 63, 64 to 127 and so on) no expert is named by more than 64 rows.
All inputs are finite; a program needn't handle non-finite values. No bound on the sum of `lengths` on one device may be relied on, other than what follows from the above.
Results may differ from a plain program's by a relative error of at most 0.0051.
Values may be sent and summed in bfloat16 or wider, within the bound.
No kernel may reach another device: no remote copies, remote signals or barrier semaphores. Data moves between devices by JAX's collectives and lax.ppermute only.
A program may use at most 192 MiB of HBM per device.

v0:
```python
import jax
import jax.numpy as jnp
from jax import lax
from jax.sharding import PartitionSpec as P

masked_score = -1e30
norm_epsilon = 1e-06


def normalize(value_sums, row_totals, heads_local):
    lead = value_sums.shape[:2]
    shaped = value_sums.reshape(lead[0], lead[1], heads_local, -1) / row_totals[..., None]
    return shaped.reshape(lead[0], lead[1], -1).astype(jnp.bfloat16)


def local(
    queries,
    new_keys,
    new_values,
    key_cache,
    value_cache,
    lengths,
    residual,
    out_weight,
    norm_gain,
    route_ids,
    route_weights,
    expert_in,
    expert_out,
):
    req_count, cache_span, kv_local, head_size = key_cache.shape
    heads_local = queries.shape[2]
    group_size = heads_local // kv_local
    score_scale = head_size ** (-0.5)
    whole_queries = lax.all_gather(queries, "exp", axis=1, tiled=True)
    block_rows = whole_queries.shape[1]
    grouped = whole_queries.reshape(req_count, block_rows, kv_local, group_size, head_size)
    cache_scores = (
        jnp.einsum("rbkgd,rskd->rkgbs", grouped, key_cache, preferred_element_type=jnp.float32)
        * score_scale
    )
    fresh_scores = (
        jnp.einsum("rbkgd,rnkd->rkgbn", grouped, new_keys, preferred_element_type=jnp.float32)
        * score_scale
    )
    positions = lax.axis_index("exp") * cache_span + lax.iota(jnp.int32, cache_span)
    valid_cache = positions[None, :] < lengths[:, None]
    cache_scores = jnp.where(valid_cache[:, None, None, None, :], cache_scores, masked_score)
    local_max = jnp.maximum(jnp.max(cache_scores, axis=-1), jnp.max(fresh_scores, axis=-1))
    row_max = lax.pmax(local_max, "exp")
    cache_exp = jnp.exp(cache_scores - row_max[..., None])
    fresh_exp = jnp.exp(fresh_scores - row_max[..., None])
    totals = jnp.sum(cache_exp, axis=-1) + jnp.sum(fresh_exp, axis=-1)
    weighted = jnp.einsum(
        "rkgbs,rskd->rbkgd",
        cache_exp.astype(jnp.bfloat16),
        value_cache,
        preferred_element_type=jnp.float32,
    )
    weighted = weighted + jnp.einsum(
        "rkgbn,rnkd->rbkgd",
        fresh_exp.astype(jnp.bfloat16),
        new_values,
        preferred_element_type=jnp.float32,
    )
    weighted = weighted.reshape(req_count, block_rows, heads_local * head_size)
    totals = jnp.transpose(totals, (0, 3, 1, 2)).reshape(req_count, block_rows, heads_local)
    all_sums, all_totals = lax.psum((weighted, totals), "exp")
    merged = normalize(all_sums, all_totals, heads_local)
    projected = jnp.dot(
        merged.reshape(req_count * block_rows, -1), out_weight, preferred_element_type=jnp.float32
    )
    projected = projected.reshape(req_count, block_rows, -1)
    projected = lax.psum(projected, "head")
    projected = projected.reshape(req_count * block_rows, projected.shape[-1])
    attn_out = lax.all_to_all(projected, "exp", split_axis=0, concat_axis=1, tiled=True)
    hidden = residual.astype(jnp.float32) + attn_out
    normed = (
        hidden
        * lax.rsqrt(jnp.mean(hidden * hidden, axis=-1, keepdims=True) + norm_epsilon)
        * norm_gain
    ).astype(jnp.bfloat16)
    row_count, model_width = normed.shape
    top_count = route_ids.shape[1]
    local_experts = expert_in.shape[0]
    groups = lax.axis_size("req") * lax.axis_size("exp")
    experts_all = local_experts * groups
    capacity = max(2, 2 * row_count * top_count // experts_all)
    expert_iota = lax.iota(jnp.int32, experts_all)
    named_count = jnp.sum((route_ids[:, :, None] == expert_iota).astype(jnp.int32), axis=1)
    earlier = jnp.cumsum(named_count, axis=0) - named_count
    slot_rank = jnp.take_along_axis(earlier, route_ids, axis=1)
    slot_index = route_ids * capacity + slot_rank
    slot_iota = lax.iota(jnp.int32, experts_all * capacity)
    placing = jnp.any(slot_index[None, :, :] == slot_iota[:, None, None], axis=2).astype(
        jnp.bfloat16
    )
    outgoing = jnp.dot(placing, normed, preferred_element_type=jnp.float32).astype(jnp.bfloat16)
    outgoing = outgoing.reshape(groups, local_experts, capacity, model_width)
    input_maps = expert_in.reshape(local_experts, model_width, -1)
    gate_up = jnp.einsum(
        "geci,eif->gecf",
        lax.all_to_all(outgoing, ("req", "exp"), split_axis=0, concat_axis=0, tiled=True),
        input_maps,
        preferred_element_type=jnp.float32,
    )
    half_units = gate_up.shape[-1] // 2
    activated = (jax.nn.silu(gate_up[..., :half_units]) * gate_up[..., half_units:]).astype(
        jnp.bfloat16
    )
    partial_value = jnp.einsum(
        "gecf,efi->geci", activated, expert_out, preferred_element_type=jnp.float32
    )
    half_width = model_width // lax.axis_size("head")
    head_start = lax.axis_index("head") * half_width
    summed = lax.psum_scatter(partial_value, "head", scatter_dimension=3, tiled=True).astype(
        jnp.bfloat16
    )
    returned = lax.all_to_all(summed, ("req", "exp"), split_axis=0, concat_axis=0, tiled=True)
    flat_results = returned.reshape(experts_all * capacity, half_width)
    picked = jnp.take(flat_results, slot_index, axis=0).astype(jnp.float32)
    mixture = jnp.sum(picked * route_weights[:, :, None], axis=1)
    kept_hidden = lax.dynamic_slice_in_dim(hidden, head_start, half_width, 1)
    return (kept_hidden + mixture).astype(jnp.bfloat16)


def solution(mesh):
    return jax.shard_map(
        local,
        mesh=mesh,
        in_specs=(
            P("req", "exp", "head", None),
            P("req", "exp", "head", None),
            P("req", "exp", "head", None),
            P("req", "exp", "head", None),
            P("req", "exp", "head", None),
            P("req"),
            P(("req", "exp"), None),
            P("head", "exp"),
            P(),
            P(("req", "exp"), None),
            P(("req", "exp"), None),
            P(("req", "exp"), None, None, "head"),
            P(("req", "exp"), "head", None),
        ),
        out_specs=P(("req", "exp"), "head"),
        check_vma=False,
    )
```

profile of v0, /device:TPU:12, one launch (start us, length us, event | category | flops | bytes accessed | tf_op | source)
XLA Modules:
  0.0 454.6 jit_solution(866792332036703675)
XLA Ops:
  8.1 28.7 %all-gather.2.cloned.1.call-done = bf16[4,64,16,128]{3,2,1,0:T(8,128)(2,1)} async-done(((bf16[4,16,16,128]{3,2,1,0:T(8,128)(2,1)}), bf16[4,64,16,128]{3,2,1,0:T(8,128)(2,1)}) %all-gather.2.cloned.1.call-update) | async-done | bytes 1048592 | tf_op jit(solution)/shard_map/all_gather | solution.py:35
  36.8 1.5 copy.79
  38.3 2.5 fusion.33
  40.8 43.4 %bitcast_reduce_fusion = (f32[4,2,8,64]{3,2,1,0:T(8,128)S(1)}, f32[4,2,6144,64,8]{2,3,4,1,0:T(8,128)}) fusion(pred[4,6144]{1,0:T(4,128)(4,1)S(1)} %broadcast_compare_fusion, bf16[4,64,2,8,128]{4,1,3,2,0:T(8,128)(2,1)S(1)} %bitcast.78, bf16[4,6144,2,128,1]{3,2,1,0,4:T(2,128)(2,1)} %bitcast.76), kind=kOutput, calls=%fused_computation.3 | convolution fusion | flops 6517944320 | bytes 114335744 | tf_op jit(solution)/shard_map/rbkgd,rskd->rkgbs/dot_general | solution.py:39
  84.2 15.3 %pmax.7 = f32[4,2,8,64]{3,2,1,0:T(8,128)S(1)} all-reduce(f32[4,2,8,64]{3,2,1,0:T(8,128)S(1)} %max.5), channel_id=1, replica_groups=mesh['req'=4,'head'=2,'exp'=4] {'exp'}, use_global_device_ids=true, to_apply=%region_2.3 | all-reduce | flops 4096 | bytes 32768 | tf_op jit(solution)/shard_map/pmax | solution.py:50
  99.5 38.4 %fusion.3 = f32[4,2,8,64,128]{4,3,2,1,0:T(8,128)} fusion(f32[4,2,6144,64,8]{2,3,4,1,0:T(8,128)} %get-tuple-element.10, f32[4,2,8,64]{3,2,1,0:T(8,128)S(1)} %pmax.7, pred[4,6144]{1,0:T(4,128)(4,1)S(1)} %broadcast_compare_fusion, bf16[4,6144,2,128,1]{3,2,1,0,4:T(2,128)(2,1)} %bitcast.83), kind=kOutput, calls=%fused_computation.8 | convolution fusion | flops 6543114240 | bytes 115384320 | tf_op jit(solution)/shard_map/rkgbs,rskd->rbkgd/dot_general | solution.py:54
  138.0 2.1 add_bitcast_fusion
  140.1 2.5 copy.84
  142.6 2.7 reshape.99
  145.4 32.4 %fusion.1 = f32[4,2,8,64]{3,2,1,0:T(8,128)S(1)} fusion(f32[4,2,6144,64,8]{2,3,4,1,0:T(8,128)} %get-tuple-element.10, f32[4,2,8,64]{3,2,1,0:T(8,128)S(1)} %pmax.7, pred[4,6144]{1,0:T(4,128)(4,1)S(1)} %broadcast_compare_fusion), kind=kLoop, calls=%fused_computation.6 | loop fusion | flops 100659200 | bytes 100720640 | tf_op jit(solution)/shard_map/reduce_sum | solution.py:53
  177.9 14.9 %psum.22 = f32[4,64,16]{1,2,0:T(8,128)S(1)} all-reduce(f32[4,64,16]{1,2,0:T(8,128)S(1)} %add_bitcast_fusion.1), channel_id=1, replica_groups=mesh['req'=4,'head'=2,'exp'=4] {'exp'}, use_global_device_ids=true, to_apply=%region_6.7 | all-reduce | flops 4096 | bytes 32768 | tf_op jit(solution)/shard_map/psum | solution.py:68
  192.9 1.9 div.21
  194.8 2.7 div.22
  197.6 17.7 %all-reduce.3.cloned.1.call-done = f32[4,64,2048]{2,1,0:T(8,128)} async-done(((f32[4,64,2048]{2,1,0:T(8,128)}), f32[4,64,2048]{2,1,0:T(8,128)}) %all-reduce.3.cloned.1.call-update) | async-done | bytes 2097168 | tf_op jit(solution)/shard_map/psum | solution.py:68
  215.3 3.7 fusion.11
  219.1 19.2 %all-reduce.5.cloned.1.call-done = f32[4,64,512]{2,1,0:T(8,128)} async-done(((f32[4,64,512]{2,1,0:T(8,128)}), f32[4,64,512]{2,1,0:T(8,128)}) %all-reduce.5.cloned.1.call-update) | async-done | bytes 524304 | tf_op jit(solution)/shard_map/psum | solution.py:74
  238.2 4.2 all-to-all-start
  242.8 3.8 gather_fusion.1
  247.6 2.8 all-to-all-done
  250.6 0.8 copy-done.2
  251.4 3.3 convolution_convert_fusion
  254.7 6.1 %all-to-all-start.1 = ((bf16[16,1,64,2048]{3,2,1,0:T(8,128)(2,1)}), bf16[16,1,64,2048]{3,2,1,0:T(8,128)(2,1)}, u32[]{:S(2)}, u32[]{:S(2)}) async-start(bf16[16,1,64,2048]{3,2,1,0:T(8,128)(2,1)} %bitcast.75), calls=%async_computation.1 | async-start | bytes 8388608 | tf_op jit(solution)/shard_map/all_to_all | solution.py:103
  260.8 8.1 %reshape.134 = bf16[2048,768,1]{1,0,2:T(8,128)(2,1)} reshape(bf16[1,2048,2,384]{3,2,1,0:T(2,128)(2,1)} %param.24) | data formatting | bytes 6291456 | tf_op jit(solution)/shard_map/reshape.3
  268.9 84.6 %all-to-all-done.1 = bf16[16,1,64,2048]{3,2,1,0:T(8,128)(2,1)} async-done(((bf16[16,1,64,2048]{3,2,1,0:T(8,128)(2,1)}), bf16[16,1,64,2048]{3,2,1,0:T(8,128)(2,1)}, u32[]{:S(2)}, u32[]{:S(2)}) %all-to-all-start.1) | async-done | bytes 4194336 | tf_op jit(solution)/shard_map/all_to_all | solution.py:103
  353.5 6.3 %fusion.14 = f32[16,1,64,768]{3,2,0,1:T(8,128)S(1)} fusion(bf16[2048,768,1]{1,0,2:T(8,128)(2,1)} %reshape.134, bf16[16,1,64,2048]{3,2,1,0:T(8,128)(2,1)} %all-to-all-done.1), kind=kOutput, calls=%fused_computation.25 | convolution fusion | flops 3221225472 | bytes 10485760 | tf_op jit(solution)/shard_map/geci,eif->gecf/dot_general | solution.py:101
  359.8 5.6 %convolution_bitcast_fusion = f32[16,1,64,2048]{3,2,0,1:T(8,128)} fusion(bf16[1,384,2048]{2,1,0:T(8,128)(2,1)S(1)} %copy-done.8, f32[16,1,64,768]{3,2,0,1:T(8,128)S(1)} %fusion.14), kind=kOutput, calls=%fused_computation.13 | convolution fusion | flops 1612972032 | bytes 13107200 | tf_op jit(solution)/shard_map/gecf,efi->geci/dot_general | solution.py:111
  365.4 16.2 %reduce-scatter.2.cloned.1.call-done = f32[16,1,64,1024]{3,2,0,1:T(8,128)} async-done(((f32[16,1,64,2048]{3,2,0,1:T(8,128)}), f32[16,1,64,1024]{3,2,0,1:T(8,128)}) %reduce-scatter.2.cloned.1.call-update) | async-done | bytes 4194320 | tf_op jit(solution)/shard_map/reduce_scatter | solution.py:116
  381.6 3.9 convert_bitcast_fusion
  385.5 7.1 %all-to-all-start.2 = ((bf16[16,1,64,1024]{3,2,1,0:T(8,128)(2,1)}), bf16[16,1,64,1024]{3,2,1,0:T(8,128)(2,1)}, u32[]{:S(2)}, u32[]{:S(2)}) async-start(bf16[16,1,64,1024]{3,2,1,0:T(8,128)(2,1)} %convert_bitcast_fusion), calls=%async_computation.3 | async-start | bytes 4194304 | tf_op jit(solution)/shard_map/all_to_all | solution.py:119
  393.0 48.1 %all-to-all-done.2 = bf16[16,1,64,1024]{3,2,1,0:T(8,128)(2,1)} async-done(((bf16[16,1,64,1024]{3,2,1,0:T(8,128)(2,1)}), bf16[16,1,64,1024]{3,2,1,0:T(8,128)(2,1)}, u32[]{:S(2)}, u32[]{:S(2)}) %all-to-all-start.2) | async-done | bytes 2097184 | tf_op jit(solution)/shard_map/all_to_all | solution.py:119
  441.0 4.6 %gather_fusion = bf16[512,1024]{1,0:T(8,128)(2,1)S(1)} fusion(bf16[1024,1024]{1,0:T(8,128)(2,1)} %bitcast.28, s32[1024]{0:T(1024)S(1)} %pad_clamp_fusion), kind=kCustom, calls=%fused_computation | custom fusion | bytes 2099200 | tf_op jit(solution)/shard_map/jit(_take)/gather | solution.py:121
  446.5 1.6 add_convert_fusion
  (53 shorter events, 4.7 us)
Async XLA Ops:
  6.5 208.7 %copy-start = (bf16[2048,512]{1,0:T(8,128)(2,1)S(1)}, bf16[2048,512]{1,0:T(8,128)(2,1)}, u32[]{:S(2)}) copy-start(bf16[2048,512]{1,0:T(8,128)(2,1)} %param.20) | copy-start | bytes 6291460
  6.5 30.3 %all-gather.2.cloned.1.call-start = ((), (), s32[]{:S(2)}) async-start(), calls=%async_computation.4 | async-start | bytes 1310720 | tf_op jit(solution)/shard_map/all_gather | solution.py:35
  7.3 208.0 %all-reduce.3.cloned.1.call-start = ((), (), s32[]{:S(2)}) async-start(), calls=%async_computation.5 | async-start | bytes 4194304 | tf_op jit(solution)/shard_map/psum | solution.py:68
  99.5 38.4 %copy-start.1 = (f32[4,2,8,64,16]{3,4,2,1,0:T(8,128)S(1)}, f32[4,2,8,64,16]{3,4,2,1,0:T(8,128)}, u32[]{:S(2)}) copy-start(f32[4,2,8,64,16]{3,4,2,1,0:T(8,128)} %get-tuple-element.12) | copy-start | bytes 786436
  99.5 38.4 %copy-start.5 = (bf16[4,16,2,128]{3,2,1,0:T(2,128)(2,1)S(1)}, bf16[4,16,2,128]{3,2,1,0:T(2,128)(2,1)}, u32[]{:S(2)}) copy-start(bf16[4,16,2,128]{3,2,1,0:T(2,128)(2,1)} %param.15) | copy-start | bytes 98308
  145.3 92.9 %all-reduce.5.cloned.1.call-start = ((), (), s32[]{:S(2)}) async-start(), calls=%async_computation.6 | async-start | bytes 1048576 | tf_op jit(solution)/shard_map/psum | solution.py:74
  197.6 21.5 %copy-start.4 = (s32[64,8]{0,1:T(8,128)S(1)}, s32[64,8]{0,1:T(8,128)}, u32[]{:S(2)}) copy-start(s32[64,8]{0,1:T(8,128)} %param.22) | copy-start | bytes 6148
  238.2 12.2 %all-to-all-start = ((f32[4,64,512]{2,1,0:T(8,128)}), f32[4,64,512]{2,1,0:T(8,128)S(1)}, u32[]{:S(2)}, u32[]{:S(2)}) async-start(f32[4,64,512]{2,1,0:T(8,128)} %all-reduce.5.cloned.1.call-done), calls=%async_computation | async-start | bytes 1048576 | tf_op jit(solution)/shard_map/all_to_all | solution.py:76
  242.8 7.6 %copy-start.3 = (bf16[64,2048]{1,0:T(8,128)(2,1)S(1)}, bf16[64,2048]{1,0:T(8,128)(2,1)}, u32[]{:S(2)}) copy-start(bf16[64,2048]{1,0:T(8,128)(2,1)} %param.19) | copy-start | bytes 786436
  242.8 8.6 %copy-start.6 = (f32[2048]{0:T(1024)S(1)}, f32[2048]{0:T(1024)}, u32[]{:S(2)}) copy-start(f32[2048]{0:T(1024)} %param.21) | copy-start | bytes 24580
  250.6 0.8 copy-start.2
  254.7 98.8 %all-to-all-start.1 = ((bf16[16,1,64,2048]{3,2,1,0:T(8,128)(2,1)}), bf16[16,1,64,2048]{3,2,1,0:T(8,128)(2,1)}, u32[]{:S(2)}, u32[]{:S(2)}) async-start(bf16[16,1,64,2048]{3,2,1,0:T(8,128)(2,1)} %bitcast.75), calls=%async_computation.1 | async-start | bytes 8388608 | tf_op jit(solution)/shard_map/all_to_all | solution.py:103
  260.8 120.8 %reduce-scatter.2.cloned.1.call-start = ((), (), s32[]{:S(2)}) async-start(), calls=%async_computation.7 | async-start | bytes 12582912 | tf_op jit(solution)/shard_map/reduce_scatter | solution.py:116
  353.5 6.3 %copy-start.8 = (bf16[1,384,2048]{2,1,0:T(8,128)(2,1)S(1)}, bf16[1,384,2048]{2,1,0:T(8,128)(2,1)}, u32[]{:S(2)}) copy-start(bf16[1,384,2048]{2,1,0:T(8,128)(2,1)} %param.25) | copy-start | bytes 4718596
  385.5 7.4 %copy-start.7 = (f32[64,8]{0,1:T(8,128)S(1)}, f32[64,8]{0,1:T(8,128)}, u32[]{:S(2)}) copy-start(f32[64,8]{0,1:T(8,128)} %param.23) | copy-start | bytes 6148
  385.5 55.6 %all-to-all-start.2 = ((bf16[16,1,64,1024]{3,2,1,0:T(8,128)(2,1)}), bf16[16,1,64,1024]{3,2,1,0:T(8,128)(2,1)}, u32[]{:S(2)}, u32[]{:S(2)}) async-start(bf16[16,1,64,1024]{3,2,1,0:T(8,128)(2,1)} %convert_bitcast_fusion), calls=%async_computation.3 | async-start | bytes 4194304 | tf_op jit(solution)/shard_map/all_to_all | solution.py:119
Sparse Core Ops, SparseCore 0:
  9.2 27.5 all-gather.1
  145.4 69.7 all-reduce.2
  219.2 19.0 all-reduce.4
  365.6 15.9 reduce-scatter.1
where the time goes:
time: 456 us; the launch traced here: 455 us
  waiting for transfers between devices  218 us (48%)
  matrix products  105 us (23%)
  other arithmetic  40.7 us (9%)
  blocking collectives  30.2 us (7%)
  local copies, waits for them, and re-layouts  29.6 us (6%)
  starting transfers between devices  17.5 us (4%)
  between operations  13.3 us (3%)
    all_to_all x1, waiting for transfers between devices, local(): lax.all_to_all(outgoing, ('req', 'exp'), split_axis=0, concat_axis=0, til...  84.6 us
    all_to_all x1, waiting for transfers between devices, local(): lax.all_to_all(summed, ('req', 'exp'), split_axis=0, concat_axis=0, tiled...  48.1 us
    dot_general x1, matrix products, local(): jnp.einsum('rbkgd,rskd->rkgbs', grouped, key_cache, preferred_element_typ...  43.4 us
    dot_general x1, matrix products, local(): jnp.einsum('rkgbs,rskd->rbkgd', cache_exp.astype(jnp.bfloat16), value_cac...  38.4 us
    reduce_sum x2, other arithmetic, local(): totals = jnp.sum(cache_exp, axis=-1) + jnp.sum(fresh_exp, axis=-1)  32.6 us
    all_gather x1, waiting for transfers between devices, local(): whole_queries = lax.all_gather(queries, 'exp', axis=1, tiled=True)  28.7 us
    psum x1, waiting for transfers between devices, local(): projected = lax.psum(projected, 'head')  19.2 us
    psum x1, waiting for transfers between devices, local(): all_sums, all_totals = lax.psum((weighted, totals), 'exp')  17.7 us
  transfers between devices with their start and end apart: 7, of which 7 were waited for; matrix products, arithmetic and copies ran while one was open for 11% of the time, Pallas kernels for 0%

commit v1 on v0

--- a/solution.py
+++ b/solution.py
@@ -32,7 +32,10 @@
     heads_local = queries.shape[2]
     group_size = heads_local // kv_local
     score_scale = head_size ** (-0.5)
-    whole_queries = lax.all_gather(queries, "exp", axis=1, tiled=True)
+    devices = lax.axis_size("exp")
+    pieces = jnp.stack([queries for _ in range(devices)])
+    pieces = lax.all_to_all(pieces, "exp", split_axis=0, concat_axis=0)
+    whole_queries = jnp.concatenate(pieces, axis=1)
     block_rows = whole_queries.shape[1]
     grouped = whole_queries.reshape(req_count, block_rows, kv_local, group_size, head_size)
     cache_scores = (

time: 456 us -> 445 us (0.976)
  waiting for transfers between devices: 218 us -> 202 us
    all_gather x1 -> x0, waiting for transfers between devices: 28.7 us -> none  [local(): whole_queries = lax.all_gather(queries, 'exp', axis=1, tiled=True)]
    all_to_all x0 -> x1, waiting for transfers between devices: none -> 13 us  [local(): pieces = lax.all_to_all(pieces, 'exp', split_axis=0, concat_axis=0)]
    another operation x1 -> x2, local copies, waits for them, and re-layouts: 8.06 us -> 9.25 us
where the time goes in v1:
time: 445 us
  waiting for transfers between devices  202 us (45%)
  matrix products  105 us (24%)
  other arithmetic  40 us (9%)
  local copies, waits for them, and re-layouts  33 us (7%)
  blocking collectives  30.2 us (7%)
  starting transfers between devices  21.8 us (5%)
  between operations  13.3 us (3%)
    all_to_all x1, waiting for transfers between devices, local(): lax.all_to_all(outgoing, ('req', 'exp'), split_axis=0, concat_axis=0, til...  84.6 us
    all_to_all x1, waiting for transfers between devices, local(): lax.all_to_all(summed, ('req', 'exp'), split_axis=0, concat_axis=0, tiled...  48.1 us
    dot_general x1, matrix products, local(): jnp.einsum('rbkgd,rskd->rkgbs', grouped, key_cache, preferred_element_typ...  43.4 us
    dot_general x1, matrix products, local(): jnp.einsum('rkgbs,rskd->rbkgd', cache_exp.astype(jnp.bfloat16), value_cac...  38.4 us
    reduce_sum x2, other arithmetic, local(): totals = jnp.sum(cache_exp, axis=-1) + jnp.sum(fresh_exp, axis=-1)  32.5 us
    psum x1, waiting for transfers between devices, local(): projected = lax.psum(projected, 'head')  19.2 us
    psum x1, waiting for transfers between devices, local(): all_sums, all_totals = lax.psum((weighted, totals), 'exp')  17.7 us
    reduce_scatter x1, waiting for transfers between devices, local(): lax.psum_scatter(partial_value, 'head', scatter_dimension=3, tiled=True)  16.2 us
  transfers between devices with their start and end apart: 7, of which 7 were waited for; matrix products, arithmetic and copies ran while one was open for 11% of the time, Pallas kernels for 0%

profile of v1, /device:TPU:12, one launch (start us, length us, event | category | flops | bytes accessed | tf_op | source)
XLA Modules:
  0.0 444.5 jit_solution(2841263396190597828)
XLA Ops:
  8.9 4.2 all-to-all-start
  13.3 13.0 %all-to-all-done = bf16[4,4,16,16,128]{4,2,3,1,0:T(8,128)(2,1)S(1)} async-done(((bf16[4,4,16,16,128]{4,2,3,1,0:T(8,128)(2,1)}), bf16[4,4,16,16,128]{4,2,3,1,0:T(8,128)(2,1)S(1)}, u32[]{:S(2)}, u32[]{:S(2)}) %all-to-all-start) | async-done | bytes 1048608 | tf_op jit(solution)/shard_map/all_to_all | solution.py:37
  27.2 1.5 copy.82
  28.8 1.8 fusion.33
  30.5 43.4 %bitcast_reduce_fusion = (f32[4,2,8,64]{3,2,1,0:T(8,128)S(1)}, f32[4,2,6144,64,8]{2,3,4,1,0:T(8,128)}) fusion(pred[4,6144]{1,0:T(4,128)(4,1)S(1)} %broadcast_compare_fusion, bf16[4,64,2,8,128]{4,1,3,2,0:T(8,128)(2,1)S(1)} %bitcast.79, bf16[4,6144,2,128,1]{3,2,1,0,4:T(2,128)(2,1)} %bitcast.77), kind=kOutput, calls=%fused_computation.3 | convolution fusion | flops 6517944320 | bytes 114335744 | tf_op jit(solution)/shard_map/rbkgd,rskd->rkgbs/dot_general | solution.py:42
  73.9 15.3 %pmax.7 = f32[4,2,8,64]{3,2,1,0:T(8,128)S(1)} all-reduce(f32[4,2,8,64]{3,2,1,0:T(8,128)S(1)} %max.5), channel_id=1, replica_groups=mesh['req'=4,'head'=2,'exp'=4] {'exp'}, use_global_device_ids=true, to_apply=%region_2.3 | all-reduce | flops 4096 | bytes 32768 | tf_op jit(solution)/shard_map/pmax | solution.py:53
  89.3 38.4 %fusion.3 = f32[4,2,8,64,128]{4,3,2,1,0:T(8,128)} fusion(f32[4,2,6144,64,8]{2,3,4,1,0:T(8,128)} %get-tuple-element.10, f32[4,2,8,64]{3,2,1,0:T(8,128)S(1)} %pmax.7, pred[4,6144]{1,0:T(4,128)(4,1)S(1)} %broadcast_compare_fusion, bf16[4,6144,2,128,1]{3,2,1,0,4:T(2,128)(2,1)} %bitcast.85), kind=kOutput, calls=%fused_computation.8 | convolution fusion | flops 6543114240 | bytes 115384320 | tf_op jit(solution)/shard_map/rkgbs,rskd->rbkgd/dot_general | solution.py:57
  127.7 2.1 add_bitcast_fusion
  129.8 2.5 copy.87
  132.3 2.7 reshape.101
  135.3 32.4 %fusion.1 = f32[4,2,8,64]{3,2,1,0:T(8,128)S(1)} fusion(f32[4,2,6144,64,8]{2,3,4,1,0:T(8,128)} %get-tuple-element.10, f32[4,2,8,64]{3,2,1,0:T(8,128)S(1)} %pmax.7, pred[4,6144]{1,0:T(4,128)(4,1)S(1)} %broadcast_compare_fusion), kind=kLoop, calls=%fused_computation.6 | loop fusion | flops 100659200 | bytes 100720640 | tf_op jit(solution)/shard_map/reduce_sum | solution.py:56
  167.8 14.9 %psum.22 = f32[4,64,16]{1,2,0:T(8,128)S(1)} all-reduce(f32[4,64,16]{1,2,0:T(8,128)S(1)} %add_bitcast_fusion.1), channel_id=1, replica_groups=mesh['req'=4,'head'=2,'exp'=4] {'exp'}, use_global_device_ids=true, to_apply=%region_6.7 | all-reduce | flops 4096 | bytes 32768 | tf_op jit(solution)/shard_map/psum | solution.py:71
  182.8 1.9 div.21
  184.8 2.7 div.22
  187.5 17.7 %all-reduce.3.cloned.1.call-done = f32[4,64,2048]{2,1,0:T(8,128)} async-done(((f32[4,64,2048]{2,1,0:T(8,128)}), f32[4,64,2048]{2,1,0:T(8,128)}) %all-reduce.3.cloned.1.call-update) | async-done | bytes 2097168 | tf_op jit(solution)/shard_map/psum | solution.py:71
  205.2 3.7 fusion.11
  209.0 19.2 %all-reduce.5.cloned.1.call-done = f32[4,64,512]{2,1,0:T(8,128)} async-done(((f32[4,64,512]{2,1,0:T(8,128)}), f32[4,64,512]{2,1,0:T(8,128)}) %all-reduce.5.cloned.1.call-update) | async-done | bytes 524304 | tf_op jit(solution)/shard_map/psum | solution.py:77
  228.1 4.2 all-to-all-start.1
  232.7 3.8 gather_fusion.1
  237.5 2.8 all-to-all-done.1
  241.3 3.3 convolution_convert_fusion
  244.6 6.1 %all-to-all-start.2 = ((bf16[16,1,64,2048]{3,2,1,0:T(8,128)(2,1)}), bf16[16,1,64,2048]{3,2,1,0:T(8,128)(2,1)}, u32[]{:S(2)}, u32[]{:S(2)}) async-start(bf16[16,1,64,2048]{3,2,1,0:T(8,128)(2,1)} %bitcast.76), calls=%async_computation.2 | async-start | bytes 8388608 | tf_op jit(solution)/shard_map/all_to_all | solution.py:106
  250.7 8.1 %reshape.136 = bf16[2048,768,1]{1,0,2:T(8,128)(2,1)} reshape(bf16[1,2048,2,384]{3,2,1,0:T(2,128)(2,1)} %param.24) | data formatting | bytes 6291456 | tf_op jit(solution)/shard_map/reshape.4
  258.8 84.6 %all-to-all-done.2 = bf16[16,1,64,2048]{3,2,1,0:T(8,128)(2,1)} async-done(((bf16[16,1,64,2048]{3,2,1,0:T(8,128)(2,1)}), bf16[16,1,64,2048]{3,2,1,0:T(8,128)(2,1)}, u32[]{:S(2)}, u32[]{:S(2)}) %all-to-all-start.2) | async-done | bytes 4194336 | tf_op jit(solution)/shard_map/all_to_all | solution.py:106
  343.4 6.3 %fusion.14 = f32[16,1,64,768]{3,2,0,1:T(8,128)S(1)} fusion(bf16[2048,768,1]{1,0,2:T(8,128)(2,1)} %reshape.136, bf16[16,1,64,2048]{3,2,1,0:T(8,128)(2,1)} %all-to-all-done.2), kind=kOutput, calls=%fused_computation.25 | convolution fusion | flops 3221225472 | bytes 10485760 | tf_op jit(solution)/shard_map/geci,eif->gecf/dot_general | solution.py:104
  349.7 5.6 %convolution_bitcast_fusion = f32[16,1,64,2048]{3,2,0,1:T(8,128)} fusion(bf16[1,384,2048]{2,1,0:T(8,128)(2,1)S(1)} %copy-done.11, f32[16,1,64,768]{3,2,0,1:T(8,128)S(1)} %fusion.14), kind=kOutput, calls=%fused_computation.13 | convolution fusion | flops 1612972032 | bytes 13107200 | tf_op jit(solution)/shard_map/gecf,efi->geci/dot_general | solution.py:114
  355.3 16.2 %reduce-scatter.2.cloned.1.call-done = f32[16,1,64,1024]{3,2,0,1:T(8,128)} async-done(((f32[16,1,64,2048]{3,2,0,1:T(8,128)}), f32[16,1,64,1024]{3,2,0,1:T(8,128)}) %reduce-scatter.2.cloned.1.call-update) | async-done | bytes 4194320 | tf_op jit(solution)/shard_map/reduce_scatter | solution.py:119
  371.5 3.9 convert_bitcast_fusion
  375.4 7.1 %all-to-all-start.3 = ((bf16[16,1,64,1024]{3,2,1,0:T(8,128)(2,1)}), bf16[16,1,64,1024]{3,2,1,0:T(8,128)(2,1)}, u32[]{:S(2)}, u32[]{:S(2)}) async-start(bf16[16,1,64,1024]{3,2,1,0:T(8,128)(2,1)} %convert_bitcast_fusion), calls=%async_computation.4 | async-start | bytes 4194304 | tf_op jit(solution)/shard_map/all_to_all | solution.py:122
  382.9 48.1 %all-to-all-done.3 = bf16[16,1,64,1024]{3,2,1,0:T(8,128)(2,1)} async-done(((bf16[16,1,64,1024]{3,2,1,0:T(8,128)(2,1)}), bf16[16,1,64,1024]{3,2,1,0:T(8,128)(2,1)}, u32[]{:S(2)}, u32[]{:S(2)}) %all-to-all-start.3) | async-done | bytes 2097184 | tf_op jit(solution)/shard_map/all_to_all | solution.py:122
  431.0 4.6 %gather_fusion = bf16[512,1024]{1,0:T(8,128)(2,1)S(1)} fusion(bf16[1024,1024]{1,0:T(8,128)(2,1)} %bitcast.29, s32[1024]{0:T(1024)S(1)} %pad_clamp_fusion), kind=kCustom, calls=%fused_computation | custom fusion | bytes 2099200 | tf_op jit(solution)/shard_map/jit(_take)/gather | solution.py:124
  436.4 1.6 add_convert_fusion
  (60 shorter events, 7.6 us)
Async XLA Ops:
  6.5 198.6 %copy-start = (bf16[2048,512]{1,0:T(8,128)(2,1)S(1)}, bf16[2048,512]{1,0:T(8,128)(2,1)}, u32[]{:S(2)}) copy-start(bf16[2048,512]{1,0:T(8,128)(2,1)} %param.20) | copy-start | bytes 6291460
  6.5 6.6 %copy-start.10 = (s32[4]{0:T(128)S(1)}, s32[4]{0:T(128)}, u32[]{:S(2)}) copy-start(s32[4]{0:T(128)} %param.18) | copy-start | bytes 52
  6.5 22.2 %copy-start.7 = (bf16[4,16,2,128]{3,2,1,0:T(2,128)(2,1)S(1)}, bf16[4,16,2,128]{3,2,1,0:T(2,128)(2,1)}, u32[]{:S(2)}) copy-start(bf16[4,16,2,128]{3,2,1,0:T(2,128)(2,1)} %param.14) | copy-start | bytes 98308
  8.9 17.4 %all-to-all-start = ((bf16[4,4,16,16,128]{4,2,3,1,0:T(8,128)(2,1)}), bf16[4,4,16,16,128]{4,2,3,1,0:T(8,128)(2,1)S(1)}, u32[]{:S(2)}, u32[]{:S(2)}) async-start(bf16[4,4,16,16,128]{4,2,3,1,0:T(8,128)(2,1)} %stack.2), calls=%async_computation | async-start | bytes 2097152 | tf_op jit(solution)/shard_map/all_to_all | solution.py:37
  13.1 192.0 %all-reduce.3.cloned.1.call-start = ((), (), s32[]{:S(2)}) async-start(), calls=%async_computation.5 | async-start | bytes 4194304 | tf_op jit(solution)/shard_map/psum | solution.py:71
  26.3 1.0 copy-start.2
  89.2 38.4 %copy-start.1 = (f32[4,2,8,64,16]{3,4,2,1,0:T(8,128)S(1)}, f32[4,2,8,64,16]{3,4,2,1,0:T(8,128)}, u32[]{:S(2)}) copy-start(f32[4,2,8,64,16]{3,4,2,1,0:T(8,128)} %get-tuple-element.12) | copy-start | bytes 786436
  89.2 38.4 %copy-start.6 = (bf16[4,16,2,128]{3,2,1,0:T(2,128)(2,1)S(1)}, bf16[4,16,2,128]{3,2,1,0:T(2,128)(2,1)}, u32[]{:S(2)}) copy-start(bf16[4,16,2,128]{3,2,1,0:T(2,128)(2,1)} %param.15) | copy-start | bytes 98308
  135.0 93.1 %all-reduce.5.cloned.1.call-start = ((), (), s32[]{:S(2)}) async-start(), calls=%async_computation.6 | async-start | bytes 1048576 | tf_op jit(solution)/shard_map/psum | solution.py:77
  187.5 21.4 %copy-start.5 = (s32[64,8]{0,1:T(8,128)S(1)}, s32[64,8]{0,1:T(8,128)}, u32[]{:S(2)}) copy-start(s32[64,8]{0,1:T(8,128)} %param.22) | copy-start | bytes 6148
  228.1 12.2 %all-to-all-start.1 = ((f32[4,64,512]{2,1,0:T(8,128)}), f32[4,64,512]{2,1,0:T(8,128)S(1)}, u32[]{:S(2)}, u32[]{:S(2)}) async-start(f32[4,64,512]{2,1,0:T(8,128)} %all-reduce.5.cloned.1.call-done), calls=%async_computation.1 | async-start | bytes 1048576 | tf_op jit(solution)/shard_map/all_to_all | solution.py:79
  232.7 7.6 %copy-start.4 = (bf16[64,2048]{1,0:T(8,128)(2,1)S(1)}, bf16[64,2048]{1,0:T(8,128)(2,1)}, u32[]{:S(2)}) copy-start(bf16[64,2048]{1,0:T(8,128)(2,1)} %param.19) | copy-start | bytes 786436
  232.7 8.6 %copy-start.8 = (f32[2048]{0:T(1024)S(1)}, f32[2048]{0:T(1024)}, u32[]{:S(2)}) copy-start(f32[2048]{0:T(1024)} %param.21) | copy-start | bytes 24580
  240.5 0.8 copy-start.3
  244.6 98.8 %all-to-all-start.2 = ((bf16[16,1,64,2048]{3,2,1,0:T(8,128)(2,1)}), bf16[16,1,64,2048]{3,2,1,0:T(8,128)(2,1)}, u32[]{:S(2)}, u32[]{:S(2)}) async-start(bf16[16,1,64,2048]{3,2,1,0:T(8,128)(2,1)} %bitcast.76), calls=%async_computation.2 | async-start | bytes 8388608 | tf_op jit(solution)/shard_map/all_to_all | solution.py:106
  250.7 120.8 %reduce-scatter.2.cloned.1.call-start = ((), (), s32[]{:S(2)}) async-start(), calls=%async_computation.7 | async-start | bytes 12582912 | tf_op jit(solution)/shard_map/reduce_scatter | solution.py:119
  343.4 6.3 %copy-start.11 = (bf16[1,384,2048]{2,1,0:T(8,128)(2,1)S(1)}, bf16[1,384,2048]{2,1,0:T(8,128)(2,1)}, u32[]{:S(2)}) copy-start(bf16[1,384,2048]{2,1,0:T(8,128)(2,1)} %param.25) | copy-start | bytes 4718596
  375.4 7.4 %copy-start.9 = (f32[64,8]{0,1:T(8,128)S(1)}, f32[64,8]{0,1:T(8,128)}, u32[]{:S(2)}) copy-start(f32[64,8]{0,1:T(8,128)} %param.23) | copy-start | bytes 6148
  375.4 55.6 %all-to-all-start.3 = ((bf16[16,1,64,1024]{3,2,1,0:T(8,128)(2,1)}), bf16[16,1,64,1024]{3,2,1,0:T(8,128)(2,1)}, u32[]{:S(2)}, u32[]{:S(2)}) async-start(bf16[16,1,64,1024]{3,2,1,0:T(8,128)(2,1)} %convert_bitcast_fusion), calls=%async_computation.4 | async-start | bytes 4194304 | tf_op jit(solution)/shard_map/all_to_all | solution.py:122
Sparse Core Ops, SparseCore 0:
  135.2 69.9 all-reduce.2
  209.1 19.0 all-reduce.4
  355.5 15.9 reduce-scatter.1
